TPU v7x, 256 devices: a whole 4x4x8 slice. The times are simulated.
256 devices in a mesh: seq: 8 (over y, core), factor: 32 (over z, x).
Axes of the slice: x: 4, y: 4, z: 8, core: 2. Of those that a mesh axis runs over, the one named last changes fastest.
Arguments:
- out_grads: bfloat16 [16384, 28672], P('seq', 'factor'), may hold values from -6 to 6
- in_acts: bfloat16 [16384, 8192], P('seq', 'factor'), may hold values from -6 to 6
- query_grads: bfloat16 [2048, 28672], P('seq', 'factor'), may hold values from -6 to 6
- query_acts: bfloat16 [2048, 8192], P('seq', 'factor'), may hold values from -6 to 6
- output_basis: float32 [1024, 28672], P('factor'), may hold values from -0.03125 to 0.03125
- input_basis: float32 [128, 8192], replicated, may hold values from -0.0625 to 0.0625
- eigenvalues: float32 [1024, 128], P('factor'), may hold values from 0.001 to 50
- doc_ids: int32 [16384], P('seq'), may hold values from 0 to 3, as said below
- doc_lengths: int32 [32], P('seq'), may hold values from 256 to 768, as said below
Outputs:
- scores: float32 [64, 32], P('factor', 'seq')
Inputs may be any that keep to these rules, and one draw needn't show every extreme that they name: doc_ids never decrease along the tokens of a group of 2048 consecutive tokens, and document k of group g holds exactly doc_lengths[g * 4 + k] of them. `doc_lengths`: the lengths of each group's 4 documents sum to 2048.
All inputs are finite; a program needn't handle non-finite values.
Results may differ from a plain program's by a relative error of at most 0.0003.
Values sent between devices are 32-bit elements; how exact they have to be, the bound alone decides.
No kernel may reach another device: no remote copies, remote signals or barrier semaphores. Data moves between devices by JAX's collectives and lax.ppermute only.
A program may use at most 64 MiB of HBM per device.

v0:
```python
import jax
import jax.numpy as jnp
from jax import lax
from jax.sharding import PartitionSpec as P

QLEN = 32


DAMPING = 1.0


def split_up(shard, dim, peers):
    before, after = (shard.shape[:dim], shard.shape[dim + 1 :])
    return jnp.moveaxis(shard.reshape(*before, peers, -1, *after), dim, 0)


def sent_and_summed(shard, axis, dim):
    peers = lax.axis_size(axis)
    blocks = lax.all_to_all(split_up(shard, dim, peers), axis, 0, 0, tiled=True)
    return jnp.sum(blocks, axis=0)


def packed_total(arrays, axis):
    line, at, finished = (jnp.concatenate([a.reshape(-1) for a in arrays]), 0, [])
    so_far = lax.psum(line, axis)
    for a in arrays:
        finished.append(so_far[at : at + a.size].reshape(a.shape))
        at += a.size
    return tuple(finished)


def sent_to_all(shard, axis):
    copies = jnp.broadcast_to(shard, (lax.axis_size(axis), *shard.shape))
    return lax.all_to_all(copies, axis, split_axis=0, concat_axis=0, tiled=True)


def laid_out(blocks, dim):
    shape = list(blocks.shape[1:])
    shape[dim] *= blocks.shape[0]
    return jnp.moveaxis(blocks, 0, dim).reshape(shape)


def collect(shard, axis, dim):
    blocks = sent_to_all(shard, axis)
    return laid_out(blocks, dim)


def contract_first(left, right, precision):
    return lax.dot_general(
        left,
        right,
        (((0,), (0,)), ((), ())),
        precision=precision,
        preferred_element_type=jnp.float32,
    )


def contract_last(left, right, precision):
    return lax.dot_general(
        left,
        right,
        (((1,), (1,)), ((), ())),
        precision=precision,
        preferred_element_type=jnp.float32,
    )


def train_rotations(gradients, weighted_in, basis_cols):
    summed = contract_first(gradients, weighted_in, lax.Precision.HIGH)
    return sent_and_summed(
        jnp.dot(basis_cols, summed, precision=lax.Precision.HIGHEST), "factor", 0
    )


def query_rotations(gradients, weighted_in, basis_cols):
    rotated = sent_and_summed(contract_last(basis_cols, gradients, lax.Precision.HIGH), "factor", 0)
    return jnp.dot(rotated, weighted_in, precision=lax.Precision.HIGHEST)


def spread_weights(weights, rot_in):
    column_count = weights.shape[1]
    return (weights[:, :, None] * rot_in[:, None, :]).reshape(
        rot_in.shape[0], column_count * rot_in.shape[1]
    )


def local(
    out_grads,
    in_acts,
    query_grads,
    query_acts,
    output_basis,
    input_basis,
    eigenvalues,
    doc_ids,
    doc_lengths,
):
    feature_width = in_acts.shape[1]
    feature_first = lax.axis_index("factor") * feature_width
    basis_part = lax.dynamic_slice_in_dim(input_basis, feature_first, feature_width, 1)
    partial_train = contract_last(in_acts, basis_part, lax.Precision.HIGH)
    partial_query = contract_last(query_acts, basis_part, lax.Precision.HIGH)
    rot_train, rot_query = packed_total((partial_train, partial_query), "factor")
    basis_cols = lax.all_to_all(output_basis, "factor", split_axis=1, concat_axis=0, tiled=True)
    doc_count = doc_lengths.shape[0]
    local_docs = jnp.arange(doc_count, dtype=jnp.int32)
    train_weights = (doc_ids[:, None] == local_docs[None, :]).astype(
        jnp.float32
    ) / doc_lengths.astype(jnp.float32)[None, :]
    query_count = query_grads.shape[0] // QLEN
    query_owner = jnp.arange(query_grads.shape[0], dtype=jnp.int32) // QLEN
    query_weights = (
        query_owner[:, None] == jnp.arange(query_count, dtype=jnp.int32)[None, :]
    ).astype(jnp.float32) / QLEN
    train_rot = train_rotations(out_grads, spread_weights(train_weights, rot_train), basis_cols)
    query_rot = query_rotations(query_grads, spread_weights(query_weights, rot_query), basis_cols)
    local_dirs = eigenvalues.shape[0]
    inner_width = eigenvalues.shape[1]
    precond = query_rot.reshape(local_dirs, query_count, inner_width) / (
        eigenvalues[:, None, :] + DAMPING
    )
    precond = precond.reshape(local_dirs, query_count * inner_width)
    all_queries = collect(precond, "seq", 1)
    all_queries = all_queries.reshape(local_dirs, all_queries.shape[1] // inner_width, inner_width)
    partial_scores = jnp.einsum(
        "kqj,kdj->qd",
        all_queries,
        train_rot.reshape(local_dirs, doc_count, inner_width),
        precision=lax.Precision.HIGHEST,
    )
    return sent_and_summed(partial_scores, "factor", 0)


def solution(mesh):
    in_specs = (
        P("seq", "factor"),
        P("seq", "factor"),
        P("seq", "factor"),
        P("seq", "factor"),
        P("factor", None),
        P(),
        P("factor", None),
        P("seq"),
        P("seq"),
    )
    out_specs = P("factor", "seq")
    return jax.shard_map(local, mesh=mesh, in_specs=in_specs, out_specs=out_specs, check_vma=False)
```

profile of v0, /device:TPU:8, one launch (start us, length us, event | category | flops | bytes accessed | tf_op | source)
XLA Modules:
  0.0 321.3 jit_solution(3566786861452882956)
XLA Ops:
  6.5 0.0 copy-start
  6.5 4.4 %copy.60 = f32[4,32,8,896]{3,2,0,1:T(8,128)} copy(f32[4,32,8,896]{3,2,1,0:T(8,128)} %bitcast.61) | data formatting | bytes 7340032 | tf_op jit(solution)/shard_map/all_to_all | solution.py:104
  11.0 11.6 %all-to-all-start = ((f32[32,32,896]{2,0,1:T(8,128)}), f32[32,32,896]{2,0,1:T(8,128)}, u32[]{:S(2)}, u32[]{:S(2)}) async-start(f32[32,32,896]{2,0,1:T(8,128)} %bitcast.57), calls=%async_computation | async-start | bytes 7340032 | tf_op jit(solution)/shard_map/all_to_all | solution.py:104
  22.5 0.0 all-reduce.2.cloned.1.call-start
  22.6 0.0 copy-done.2
  22.6 1.1 convolution_bitcast_fusion.2
  23.7 0.1 copy.37
  23.8 0.0 copy-done
  23.8 0.0 copy-start.5
  23.9 1.7 convolution_bitcast_fusion
  25.6 0.3 copy.36
  25.9 0.0 copy-start.1
  25.9 1.2 pad_maximum_fusion
  27.1 0.0 all-reduce.2.cloned.1.call-update
  27.1 0.0 copy-done.5
  27.2 0.0 copy-start.4
  27.2 0.0 copy-start.3
  27.2 88.1 %all-to-all-done = f32[32,32,896]{2,0,1:T(8,128)} async-done(((f32[32,32,896]{2,0,1:T(8,128)}), f32[32,32,896]{2,0,1:T(8,128)}, u32[]{:S(2)}, u32[]{:S(2)}) %all-to-all-start) | async-done | bytes 3670048 | tf_op jit(solution)/shard_map/all_to_all | solution.py:104
  115.3 0.0 copy-done.1
  115.3 4.3 %fusion.3 = f32[32,32,256]{2,1,0:T(8,128)} fusion(f32[32,32,896]{2,0,1:T(8,128)} %all-to-all-done, bf16[256,896]{1,0:T(8,128)(2,1)S(1)} %copy-done.1), kind=kOutput, calls=%fused_computation.4 | convolution fusion | flops 1409286144 | bytes 5177344 | tf_op jit(solution)/shard_map/dot_general | solution.py:59
  119.6 5.2 %all-to-all-start.1 = ((f32[32,32,256]{2,1,0:T(8,128)}), f32[32,32,256]{2,1,0:T(8,128)S(1)}, u32[]{:S(2)}, u32[]{:S(2)}) async-start(f32[32,32,256]{2,1,0:T(8,128)} %fusion.3), calls=%async_computation.1 | async-start | bytes 2097152 | tf_op jit(solution)/shard_map/all_to_all | solution.py:19
  124.8 0.0 copy-done.4
  124.8 0.1 convert_divide_fusion
  124.9 0.4 copy.42
  125.3 0.0 copy-done.3
  125.3 76.9 %all-reduce.2.cloned.1.call-done = f32[294912]{0:T(1024)} async-done(((f32[294912]{0:T(1024)}), f32[294912]{0:T(1024)}) %all-reduce.2.cloned.1.call-update) | async-done | bytes 1179664 | tf_op jit(solution)/shard_map/psum | solution.py:25
  202.2 0.9 slice_bitcast_fusion.1
  203.1 0.1 copy.38
  203.2 1.3 slice_bitcast_fusion
  204.5 8.7 %broadcast_multiply_fusion = f32[2048,4,128]{2,1,0:T(4,128)} fusion(f32[2048,128]{1,0:T(8,128)S(1)} %slice_bitcast_fusion, f32[2048,4]{1,0:T(8,128)S(1)} %copy.42), kind=kLoop, calls=%fused_computation.7 | loop fusion | flops 1048576 | bytes 5275648 | tf_op jit(solution)/shard_map/mul | solution.py:82
  213.2 0.0 all-to-all-done.1
  213.2 0.1 reduce_sum.27
  213.2 1.0 fusion.5
  214.3 1.1 broadcast_in_dim.2
  215.4 4.8 %all-to-all-start.2 = ((f32[8,32,1024]{2,1,0:T(8,128)}), f32[8,32,1024]{2,1,0:T(8,128)}, u32[]{:S(2)}, u32[]{:S(2)}) async-start(f32[8,32,1024]{2,1,0:T(8,128)} %broadcast_in_dim.2), calls=%async_computation.2 | async-start | bytes 2097152 | tf_op jit(solution)/shard_map/all_to_all | solution.py:34
  220.3 7.8 %fusion = f32[512,896]{1,0:T(8,128)S(1)} fusion(bf16[2048,896]{1,0:T(8,128)(2,1)} %param.9, f32[256,8,4,128]{3,2,1,0:T(4,128)} %bitcast.58), kind=kOutput, calls=%fused_computation | convolution fusion | flops 5637144576 | bytes 9699328 | tf_op jit(solution)/shard_map/dot_general | solution.py:49
  228.1 8.9 %convolution_bitcast_fusion.1 = f32[1024,512]{0,1:T(8,128)S(1)} fusion(f32[512,896]{1,0:T(8,128)S(1)} %fusion, f32[1024,896]{1,0:T(8,128)} %bitcast.15), kind=kOutput, calls=%fused_computation.8 | convolution fusion | flops 5637144576 | bytes 7602176 | tf_op jit(solution)/shard_map/dot_general | solution.py:71
  237.0 1.9 copy.43
  238.9 0.0 all-to-all-done.2
  238.9 5.8 %all-to-all-start.3 = ((f32[32,32,512]{2,1,0:T(8,128)}), f32[32,32,512]{2,1,0:T(8,128)S(1)}, u32[]{:S(2)}, u32[]{:S(2)}) async-start(f32[32,32,512]{2,1,0:T(8,128)} %bitcast.17), calls=%async_computation.3 | async-start | bytes 4194304 | tf_op jit(solution)/shard_map/all_to_all | solution.py:19
  244.7 2.8 copy.40
  247.5 2.4 reshape_reshape.3
  249.9 45.3 %all-to-all-done.3 = f32[32,32,512]{2,1,0:T(8,128)S(1)} async-done(((f32[32,32,512]{2,1,0:T(8,128)}), f32[32,32,512]{2,1,0:T(8,128)S(1)}, u32[]{:S(2)}, u32[]{:S(2)}) %all-to-all-start.3) | async-done | bytes 2097184 | tf_op jit(solution)/shard_map/all_to_all | solution.py:19
  295.2 0.1 reduce_sum.28
  295.3 3.4 %convolution_bitcast_fusion.3 = f32[32,2,4]{0,2,1:T(4,128)S(1)} fusion(f32[32,4,128,1]{2,1,0,3:T(4,128)S(1)} %reshape.128, f32[32,2,128,32]{2,1,0,3:T(2,128)} %bitcast.59), kind=kOutput, calls=%fused_computation.13 | convolution fusion | flops 12582912 | bytes 1115136 | tf_op jit(solution)/shard_map/kqj,kdj->qd/dot_general | solution.py:125
  298.7 0.1 copy.45
  298.8 15.0 %all_to_all.39 = f32[32,2,4]{2,1,0:T(2,128)S(1)} all-to-all(f32[32,2,4]{2,1,0:T(2,128)S(1)} %copy.45), channel_id=1, replica_groups=mesh['seq'=8,'factor'=32] {'factor'}, dimensions={0} | all-to-all | bytes 2048 | tf_op jit(solution)/shard_map/all_to_all | solution.py:19
  313.8 0.6 reduce_sum.29
  (7 shorter events, 0.1 us)
Async XLA Ops:
  6.5 17.3 %copy-start = (bf16[2048,256]{1,0:T(8,128)(2,1)S(1)}, bf16[2048,256]{1,0:T(8,128)(2,1)}, u32[]{:S(2)}) copy-start(bf16[2048,256]{1,0:T(8,128)(2,1)} %param.10) | copy-start | bytes 3145732
  11.0 11.6 %copy-start.2 = (bf16[256,256]{1,0:T(8,128)(2,1)S(1)}, bf16[256,256]{1,0:T(8,128)(2,1)}, u32[]{:S(2)}) copy-start(bf16[256,256]{1,0:T(8,128)(2,1)} %param.12) | copy-start | bytes 393220
  11.0 104.3 %all-to-all-start = ((f32[32,32,896]{2,0,1:T(8,128)}), f32[32,32,896]{2,0,1:T(8,128)}, u32[]{:S(2)}, u32[]{:S(2)}) async-start(f32[32,32,896]{2,0,1:T(8,128)} %bitcast.57), calls=%async_computation | async-start | bytes 7340032 | tf_op jit(solution)/shard_map/all_to_all | solution.py:104
  22.5 179.7 %all-reduce.2.cloned.1.call-start = ((), (), s32[]{:S(2)}) async-start(), calls=%async_computation.5 | async-start | bytes 2359296 | tf_op jit(solution)/shard_map/psum | solution.py:25
  23.8 3.3 %copy-start.5 = (s32[4]{0:T(128)S(1)}, s32[4]{0:T(128)}, u32[]{:S(2)}) copy-start(s32[4]{0:T(128)} %param.17) | copy-start | bytes 52
  25.9 89.3 %copy-start.1 = (bf16[256,896]{1,0:T(8,128)(2,1)S(1)}, bf16[256,896]{1,0:T(8,128)(2,1)}, u32[]{:S(2)}) copy-start(bf16[256,896]{1,0:T(8,128)(2,1)} %param.11) | copy-start | bytes 1376260
  27.2 97.6 %copy-start.4 = (s32[2048]{0:T(1024)S(1)}, s32[2048]{0:T(1024)}, u32[]{:S(2)}) copy-start(s32[2048]{0:T(1024)} %param.16) | copy-start | bytes 24580
  27.2 98.1 %copy-start.3 = (f32[32,128]{1,0:T(8,128)S(1)}, f32[32,128]{1,0:T(8,128)}, u32[]{:S(2)}) copy-start(f32[32,128]{1,0:T(8,128)} %param.15) | copy-start | bytes 49156
  119.6 93.6 %all-to-all-start.1 = ((f32[32,32,256]{2,1,0:T(8,128)}), f32[32,32,256]{2,1,0:T(8,128)S(1)}, u32[]{:S(2)}, u32[]{:S(2)}) async-start(f32[32,32,256]{2,1,0:T(8,128)} %fusion.3), calls=%async_computation.1 | async-start | bytes 2097152 | tf_op jit(solution)/shard_map/all_to_all | solution.py:19
  215.4 23.4 %all-to-all-start.2 = ((f32[8,32,1024]{2,1,0:T(8,128)}), f32[8,32,1024]{2,1,0:T(8,128)}, u32[]{:S(2)}, u32[]{:S(2)}) async-start(f32[8,32,1024]{2,1,0:T(8,128)} %broadcast_in_dim.2), calls=%async_computation.2 | async-start | bytes 2097152 | tf_op jit(solution)/shard_map/all_to_all | solution.py:34
  238.9 56.3 %all-to-all-start.3 = ((f32[32,32,512]{2,1,0:T(8,128)}), f32[32,32,512]{2,1,0:T(8,128)S(1)}, u32[]{:S(2)}, u32[]{:S(2)}) async-start(f32[32,32,512]{2,1,0:T(8,128)} %bitcast.17), calls=%async_computation.3 | async-start | bytes 4194304 | tf_op jit(solution)/shard_map/all_to_all | solution.py:19
Sparse Core Ops, SparseCore 0:
  27.3 174.8 all-reduce.1
where the time goes:
time: 322 us; the launch traced here: 321 us
  waiting for transfers between devices  210 us (65%)
  matrix products  28.3 us (9%)
  starting transfers between devices  27.5 us (9%)
  local copies, waits for them, and re-layouts  15.9 us (5%)
  blocking collectives  15 us (5%)
  between operations  13.6 us (4%)
  other arithmetic  10.7 us (3%)
    all_to_all x1, waiting for transfers between devices, local(): lax.all_to_all(output_basis, 'factor', split_axis=1, concat_axis=0, tiled...  88.1 us
    psum x1, waiting for transfers between devices, packed_total(): so_far = lax.psum(line, axis)  76.9 us
    all_to_all x2, waiting for transfers between devices, sent_and_summed(): blocks = lax.all_to_all(split_up(shard, dim, peers), axis, 0, 0, tiled=True)  45.3 us
    all_to_all x1, blocking collectives, sent_and_summed(): blocks = lax.all_to_all(split_up(shard, dim, peers), axis, 0, 0, tiled=True)  15 us
    all_to_all x1, starting transfers between devices, local(): lax.all_to_all(output_basis, 'factor', split_axis=1, concat_axis=0, tiled...  11.6 us
    all_to_all x2, starting transfers between devices, sent_and_summed(): blocks = lax.all_to_all(split_up(shard, dim, peers), axis, 0, 0, tiled=True)  11 us
    dot_general x1, matrix products, train_rotations(): jnp.dot(basis_cols, summed, precision=lax.Precision.HIGHEST)  8.88 us
    mul x1, other arithmetic, spread_weights(): weights[:, :, None] * rot_in[:, None, :]  8.65 us
  transfers between devices with their start and end apart: 5, of which 3 were waited for; matrix products, arithmetic and copies ran while one was open for 14% of the time, Pallas kernels for 0%

commit v1 on v0

v1 whole, which is shorter than its diff:
```python
import jax
import jax.numpy as jnp
from jax import lax
from jax.sharding import Mesh, PartitionSpec as P

QLEN = 32
DAMPING = 1.0
ZX = ("z", "x")
HIGH = lax.Precision.HIGH
HIGHEST = lax.Precision.HIGHEST


def exchange(blocks, axis):
    return lax.all_to_all(blocks, axis, 0, 0, tiled=True)


def gathered(shard, axis):
    return exchange(jnp.broadcast_to(shard[None], (lax.axis_size(axis), *shard.shape)), axis)


def from_ahead(shard, axis, hops):
    n = lax.axis_size(axis)
    return lax.ppermute(shard, axis, [((i + hops) % n, i) for i in range(n)])


def dot(left, right, left_dim, right_dim, precision):
    return lax.dot_general(
        left,
        right,
        (((left_dim,), (right_dim,)), ((), ())),
        precision=precision,
        preferred_element_type=jnp.float32,
    )


def reduced_over_x(slabs):
    n = slabs.shape[-1]
    blocks = jnp.moveaxis(slabs, 1, 0).reshape(4, 256, n)
    summed = jnp.sum(exchange(blocks, "x"), axis=0)
    return jnp.moveaxis(summed.reshape(8, 8, 4, n), 1, 0).reshape(8, 32, n)


def local(
    out_grads,
    in_acts,
    query_grads,
    query_acts,
    output_basis,
    input_basis,
    eigenvalues,
    doc_ids,
    doc_lengths,
):
    y, core = lax.axis_index("y"), lax.axis_index("core")
    seq = 2 * y + core
    factor = 4 * lax.axis_index("z") + lax.axis_index("x")
    width = in_acts.shape[1]
    tokens, query_tokens = in_acts.shape[0], query_acts.shape[0]

    basis_part = lax.dynamic_slice_in_dim(input_basis, factor * width, width, 1)
    partial = jnp.concatenate(
        [dot(in_acts, basis_part, 1, 1, HIGH), dot(query_acts, basis_part, 1, 1, HIGH)], 0
    )
    inner = partial.shape[1]
    rows = partial.shape[0]
    part = jnp.sum(exchange(partial.reshape(4, rows // 4, inner), "x"), axis=0)
    part = jnp.sum(exchange(part.reshape(8, rows // 32, inner), "z"), axis=0)
    part = gathered(part, "z").reshape(rows // 4, inner)
    rot_in = gathered(part, "x").reshape(rows, inner)
    rot_train, rot_query = rot_in[:tokens], rot_in[tokens:]

    cols = output_basis.shape[1] // 32
    mine = lax.dynamic_slice_in_dim(output_basis, 4 * seq, 4, 0)
    got = exchange(jnp.moveaxis(mine.reshape(4, 32, cols), 1, 0), ZX)
    own = jnp.moveaxis(got.reshape(8, 4, 4, cols), 1, 0).reshape(128, cols)
    slabs = jnp.stack([own] + [from_ahead(own, "y", k) for k in (1, 2, 3)])
    other = from_ahead(slabs, "core", 1)
    basis_cols = jnp.concatenate([slabs, other], 0).reshape(1024, cols)

    slot = jnp.arange(32, dtype=jnp.int32)
    slot_seq = 2 * ((y + (slot // 4) % 4) % 4) + (core + slot // 16) % 2
    place = 4 * slot_seq + slot % 4
    to_order = (slot[:, None] == place[None, :]).astype(jnp.float32)

    query_count = query_tokens // QLEN
    rot = dot(basis_cols, query_grads, 1, 1, HIGH).reshape(8, 4, 8, 4, query_tokens)
    rot = jnp.sum(exchange(reduced_over_x(rot), "z"), axis=0)
    rot = dot(to_order, rot, 1, 0, HIGHEST)
    query_rot = jnp.einsum(
        "kqt,qtj->kqj",
        rot.reshape(32, query_count, QLEN),
        rot_query.reshape(query_count, QLEN, inner),
        precision=HIGHEST,
    ) * (1.0 / QLEN)
    precond = query_rot / (eigenvalues[:, None, :] + DAMPING)
    precond = gathered(precond, "y")
    precond = gathered(precond, "core")

    doc_count = doc_lengths.shape[0]
    local_docs = jnp.arange(doc_count, dtype=jnp.int32)
    weights = (doc_ids[:, None] == local_docs[None, :]).astype(jnp.float32) / doc_lengths.astype(
        jnp.float32
    )[None, :]
    spread = (weights[:, :, None] * rot_train[:, None, :]).reshape(tokens, doc_count * inner)
    summed = dot(out_grads, spread, 0, 0, HIGH)
    train = jnp.dot(basis_cols, summed, precision=HIGH).reshape(8, 4, 8, 4, doc_count * inner)
    train = jnp.sum(exchange(reduced_over_x(train), "z"), axis=0)
    train = dot(to_order, train, 1, 0, HIGHEST).reshape(32, doc_count, inner)

    partial_scores = jnp.einsum("cykqj,kdj->ycqd", precond, train, precision=HIGHEST)
    partial_scores = partial_scores.reshape(32, 2, doc_count)
    return jnp.sum(exchange(partial_scores, ZX), axis=0)


def solution(mesh):
    fine = Mesh(mesh.devices.reshape(4, 2, 8, 4), ("y", "core", "z", "x"))
    seq, factor = ("y", "core"), ("z", "x")
    in_specs = (
        P(seq, factor),
        P(seq, factor),
        P(seq, factor),
        P(seq, factor),
        P(factor, None),
        P(),
        P(factor, None),
        P(seq),
        P(seq),
    )
    return jax.shard_map(
        local, mesh=fine, in_specs=in_specs, out_specs=P(factor, seq), check_vma=False
    )
```

time: 322 us -> 244 us (0.76)
  waiting for transfers between devices: 210 us -> 83.7 us
  starting transfers between devices: 27.5 us -> 52.9 us
  blocking collectives: 15 us -> 32.6 us
  local copies, waits for them, and re-layouts: 15.9 us -> 32.7 us
  between operations: 13.6 us -> 0.42 us
  other arithmetic: 10.7 us -> 15 us
  matrix products: 28.3 us -> 24.4 us
    psum x1 -> x0, waiting for transfers between devices: 76.9 us -> none  [packed_total(): so_far = lax.psum(line, axis)]
    all_to_all x4 -> x10, waiting for transfers between devices: 133 us -> 72 us  [exchange(): return lax.all_to_all(blocks, axis, 0, 0, tiled=True)]
    all_to_all x4 -> x10, starting transfers between devices: 27.4 us -> 48 us  [exchange(): return lax.all_to_all(blocks, axis, 0, 0, tiled=True)]
    all_to_all x1 -> x2, blocking collectives: 15 us -> 32.6 us  [exchange(): return lax.all_to_all(blocks, axis, 0, 0, tiled=True)]
    ppermute x0 -> x4, waiting for transfers between devices: none -> 11.7 us  [from_ahead(): return lax.ppermute(shard, axis, [((i + hops) % n, i) for i in range(n)])]
    reshape x2 -> x8, local copies, waits for them, and re-layouts: 0.03 us -> 6.59 us  [the longest x2 3.12 us: reduced_over_x(): blocks = jnp.moveaxis(slabs, 1, 0).reshape(4, 256, n)]
    concatenate x0 -> x5, local copies, waits for them, and re-layouts: none -> 5.38 us  [the longest x4 3.98 us: local(): basis_cols = jnp.concatenate([slabs, other], 0).reshape(1024, cols)]
    unnamed x12 -> x30, local copies, waits for them, and re-layouts: 0.03 us -> 5.17 us
  transfers between devices with their start and end apart: 5 -> 14, of which waited for: 3 -> 11; matrix products, arithmetic and copies ran while one was open for 14% -> 23% of each run, Pallas kernels for 0% -> 0%
where the time goes in v1:
time: 244 us; the launch traced here: 242 us
  waiting for transfers between devices  83.7 us (34%)
  starting transfers between devices  52.9 us (22%)
  local copies, waits for them, and re-layouts  32.7 us (13%)
  blocking collectives  32.6 us (13%)
  matrix products  24.4 us (10%)
  other arithmetic  15 us (6%)
    all_to_all x10, waiting for transfers between devices, exchange(): return lax.all_to_all(blocks, axis, 0, 0, tiled=True)  72 us
    all_to_all x10, starting transfers between devices, exchange(): return lax.all_to_all(blocks, axis, 0, 0, tiled=True)  48 us
    all_to_all x2, blocking collectives, exchange(): return lax.all_to_all(blocks, axis, 0, 0, tiled=True)  32.6 us
    dot_general x6, matrix products, dot(): lax.dot_general(left, right, (((left_dim,), (right_dim,)), ((), ())), pre...  12.7 us
    ppermute x4, waiting for transfers between devices, from_ahead(): return lax.ppermute(shard, axis, [((i + hops) % n, i) for i in range(n)])  11.7 us
    mul x1, other arithmetic, local(): weights[:, :, None] * rot_train[:, None, :]  9.55 us
    dot_general x1, matrix products, local(): jnp.einsum('cykqj,kdj->ycqd', precond, train, precision=HIGHEST)  7 us
    unnamed x30, local copies, waits for them, and re-layouts  5.17 us
  transfers between devices with their start and end apart: 14, of which 11 were waited for; matrix products, arithmetic and copies ran while one was open for 23% of the time, Pallas kernels for 0%

profile of v1, /device:TPU:8, one launch (start us, length us, event | category | flops | bytes accessed | tf_op | source)
XLA Modules:
  0.0 241.8 jit_solution(3050223426544938036)
XLA Ops:
  0.0 2.1 constant_dynamic-slice_fusion
  2.1 11.3 %all-to-all-start = ((f32[32,4,896]{2,1,0:T(4,128)}), f32[32,4,896]{2,1,0:T(4,128)S(1)}, u32[]{:S(2)}, u32[]{:S(2)}) async-start(f32[32,4,896]{2,1,0:T(4,128)} %bitcast.2), calls=%async_computation | async-start | bytes 917504 | tf_op jit(solution)/shard_map/all_to_all | solution.py:14
  13.5 1.2 convolution_bitcast_fusion.2
  14.7 1.7 convolution_bitcast_fusion
  16.4 13.6 %all-to-all-done = f32[32,4,896]{2,1,0:T(4,128)S(1)} async-done(((f32[32,4,896]{2,1,0:T(4,128)}), f32[32,4,896]{2,1,0:T(4,128)S(1)}, u32[]{:S(2)}, u32[]{:S(2)}) %all-to-all-start) | async-done | bytes 458784 | tf_op jit(solution)/shard_map/all_to_all | solution.py:14
  31.7 2.6 %collective-permute-start.1 = (f32[128,896]{1,0:T(8,128)}, f32[128,896]{1,0:T(8,128)}, u32[]{:S(2)}, u32[]{:S(2)}) collective-permute-start(f32[128,896]{1,0:T(8,128)} %reshape.176), channel_id=1, source_target_pairs={{128,0},{192,64},{0,128},{64,192},{129,1},{193,65},{1,129},{65,193... | collective-permute-start | bytes 1376264 | tf_op jit(solution)/shard_map/ppermute | solution.py:23
  34.3 1.9 collective-permute-start.2
  36.2 1.4 copy.110
  37.6 3.5 %all-to-all-start.1 = ((f32[4,576,128]{2,1,0:T(8,128)}), f32[4,576,128]{2,1,0:T(8,128)S(1)}, u32[]{:S(2)}, u32[]{:S(2)}) async-start(f32[4,576,128]{2,1,0:T(8,128)} %bitcast.12), calls=%async_computation.1 | async-start | bytes 2359296 | tf_op jit(solution)/shard_map/all_to_all | solution.py:14
  41.4 2.5 %collective-permute-done = f32[128,896]{1,0:T(8,128)} collective-permute-done((f32[128,896]{1,0:T(8,128)}, f32[128,896]{1,0:T(8,128)}, u32[]{:S(2)}, u32[]{:S(2)}) %collective-permute-start) | collective-permute-done | bytes 458784 | tf_op jit(solution)/shard_map/ppermute | solution.py:23
  43.9 8.4 %collective-permute-done.1 = f32[128,896]{1,0:T(8,128)} collective-permute-done((f32[128,896]{1,0:T(8,128)}, f32[128,896]{1,0:T(8,128)}, u32[]{:S(2)}, u32[]{:S(2)}) %collective-permute-start.1) | collective-permute-done | bytes 458784 | tf_op jit(solution)/shard_map/ppermute | solution.py:23
  53.1 2.7 %pad_maximum_fusion = f32[4,128,896]{2,1,0:T(8,128)} fusion(f32[1,128,896]{2,1,0:T(8,128)} %bitcast.8, f32[1,128,896]{2,1,0:T(8,128)} %bitcast.7, f32[1,128,896]{2,1,0:T(8,128)} %bitcast.6, f32[1,128,896]{2,1,0:T(8,128)S(1)} %stack_reshape.3), kind=kLoop, calls=%fused_computation.5 | loop fusion | flops 1376256 | bytes 3670016 | tf_op jit(solution)/shard_map/stack | solution.py:76
  56.6 4.1 %all-to-all-start.2 = ((f32[8,72,128]{2,1,0:T(8,128)}), f32[8,72,128]{2,1,0:T(8,128)S(1)}, u32[]{:S(2)}, u32[]{:S(2)}) async-start(f32[8,72,128]{2,1,0:T(8,128)} %bitcast.13), calls=%async_computation.2 | async-start | bytes 589824 | tf_op jit(solution)/shard_map/all_to_all | solution.py:14
  60.7 13.2 %all-to-all-done.2 = f32[8,72,128]{2,1,0:T(8,128)S(1)} async-done(((f32[8,72,128]{2,1,0:T(8,128)}), f32[8,72,128]{2,1,0:T(8,128)S(1)}, u32[]{:S(2)}, u32[]{:S(2)}) %all-to-all-start.2) | async-done | bytes 294944 | tf_op jit(solution)/shard_map/all_to_all | solution.py:14
  74.7 3.4 %all-to-all-start.3 = ((f32[8,72,128]{2,1,0:T(8,128)}), f32[8,72,128]{2,1,0:T(8,128)S(1)}, u32[]{:S(2)}, u32[]{:S(2)}) async-start(f32[8,72,128]{2,1,0:T(8,128)} %broadcast_in_dim.10), calls=%async_computation.3 | async-start | bytes 589824 | tf_op jit(solution)/shard_map/all_to_all | solution.py:14
  79.1 1.1 concatenate.19
  80.2 1.1 concatenate.20
  81.4 1.1 concatenate.21
  84.1 7.0 %all-to-all-done.3 = f32[8,72,128]{2,1,0:T(8,128)S(1)} async-done(((f32[8,72,128]{2,1,0:T(8,128)}), f32[8,72,128]{2,1,0:T(8,128)S(1)}, u32[]{:S(2)}, u32[]{:S(2)}) %all-to-all-start.3) | async-done | bytes 294944 | tf_op jit(solution)/shard_map/all_to_all | solution.py:14
  91.1 1.2 broadcast_in_dim.12
  92.3 4.1 %all-to-all-start.4 = ((f32[4,576,128]{2,1,0:T(8,128)}), f32[4,576,128]{2,1,0:T(8,128)S(1)}, u32[]{:S(2)}, u32[]{:S(2)}) async-start(f32[4,576,128]{2,1,0:T(8,128)} %broadcast_in_dim.12), calls=%async_computation.4 | async-start | bytes 2359296 | tf_op jit(solution)/shard_map/all_to_all | solution.py:14
  97.2 2.8 %copy.104 = f32[4,128,896]{2,0,1:T(4,128)S(1)} copy(f32[4,128,896]{2,1,0:T(8,128)} %collective-permute-done.3) | data formatting | bytes 3670016 | tf_op jit(solution)/shard_map/ppermute | solution.py:23
  100.6 1.8 copy-done.2
  102.4 1.3 convolution_bitcast_fusion.1
  104.4 1.1 copy.117
  105.6 7.6 %all-to-all-done.4 = f32[4,576,128]{2,1,0:T(8,128)S(1)} async-done(((f32[4,576,128]{2,1,0:T(8,128)}), f32[4,576,128]{2,1,0:T(8,128)S(1)}, u32[]{:S(2)}, u32[]{:S(2)}) %all-to-all-start.4) | async-done | bytes 1179680 | tf_op jit(solution)/shard_map/all_to_all | solution.py:14
  113.1 3.5 %all-to-all-start.7 = ((f32[4,256,256]{2,1,0:T(8,128)}), f32[4,256,256]{2,1,0:T(8,128)S(1)}, u32[]{:S(2)}, u32[]{:S(2)}) async-start(f32[4,256,256]{2,1,0:T(8,128)} %copy.117), calls=%async_computation.7 | async-start | bytes 2097152 | tf_op jit(solution)/shard_map/all_to_all | solution.py:14
  116.7 1.3 copy.109
  118.2 9.5 %broadcast_multiply_fusion = f32[2048,4,128]{2,1,0:T(4,128)} fusion(f32[2048,128]{1,0:T(8,128)S(1)} %slice.8, f32[2048,4]{1,0:T(8,128)} %copy.109), kind=kLoop, calls=%fused_computation.4 | loop fusion | flops 1048576 | bytes 5275648 | tf_op jit(solution)/shard_map/mul | solution.py:104
  127.7 3.3 %all-to-all-done.7 = f32[4,256,256]{2,1,0:T(8,128)S(1)} async-done(((f32[4,256,256]{2,1,0:T(8,128)}), f32[4,256,256]{2,1,0:T(8,128)S(1)}, u32[]{:S(2)}, u32[]{:S(2)}) %all-to-all-start.7) | async-done | bytes 1048608 | tf_op jit(solution)/shard_map/all_to_all | solution.py:14
  132.1 3.6 %all-to-all-start.8 = ((f32[8,32,256]{2,1,0:T(8,128)}), f32[8,32,256]{2,1,0:T(8,128)S(1)}, u32[]{:S(2)}, u32[]{:S(2)}) async-start(f32[8,32,256]{2,1,0:T(8,128)} %copy.119), calls=%async_computation.8 | async-start | bytes 524288 | tf_op jit(solution)/shard_map/all_to_all | solution.py:14
  135.7 8.0 %fusion = f32[512,896]{1,0:T(8,128)S(1)} fusion(bf16[2048,896]{1,0:T(8,128)(2,1)} %param.9, f32[256,8,4,128]{3,2,1,0:T(4,128)} %bitcast.88), kind=kOutput, calls=%fused_computation | convolution fusion | flops 5637144576 | bytes 9699328 | tf_op jit(solution)/shard_map/dot_general | solution.py:27
  143.7 3.5 %fusion.5 = f32[4,8,8,4,512]{4,2,3,0,1:T(8,128)S(1)} fusion(f32[8,4,8,4,896]{4,2,3,1,0:T(8,128)S(1)} %copy-done.3, f32[512,896]{1,0:T(8,128)S(1)} %fusion), kind=kOutput, calls=%fused_computation.9 | convolution fusion | flops 2818572288 | bytes 7602176 | tf_op jit(solution)/shard_map/dot_general | solution.py:106
  147.2 1.4 copy.111
  148.6 2.0 copy.112
  150.5 3.6 %all-to-all-start.5 = ((f32[4,256,512]{2,1,0:T(8,128)}), f32[4,256,512]{2,1,0:T(8,128)S(1)}, u32[]{:S(2)}, u32[]{:S(2)}) async-start(f32[4,256,512]{2,1,0:T(8,128)} %copy.112), calls=%async_computation.5 | async-start | bytes 4194304 | tf_op jit(solution)/shard_map/all_to_all | solution.py:14
  154.2 1.6 slice.9
  156.3 1.2 fusion.9
  157.6 21.4 %all-to-all-done.5 = f32[4,256,512]{2,1,0:T(8,128)S(1)} async-done(((f32[4,256,512]{2,1,0:T(8,128)}), f32[4,256,512]{2,1,0:T(8,128)S(1)}, u32[]{:S(2)}, u32[]{:S(2)}) %all-to-all-start.5) | async-done | bytes 2097184 | tf_op jit(solution)/shard_map/all_to_all | solution.py:14
  179.8 7.0 %all-to-all-start.9 = ((f32[4,32,8,128]{3,2,1,0:T(8,128)}), f32[4,32,8,128]{3,2,1,0:T(8,128)}, u32[]{:S(2)}, u32[]{:S(2)}) async-start(f32[4,32,8,128]{3,2,1,0:T(8,128)} %broadcast_in_dim.13), calls=%async_computation.9 | async-start | bytes 1048576 | tf_op jit(solution)/shard_map/all_to_all | solution.py:14
  187.8 1.2 reshape.181
  189.4 4.0 %all-to-all-done.9 = f32[4,32,8,128]{3,2,1,0:T(8,128)} async-done(((f32[4,32,8,128]{3,2,1,0:T(8,128)}), f32[4,32,8,128]{3,2,1,0:T(8,128)}, u32[]{:S(2)}, u32[]{:S(2)}) %all-to-all-start.9) | async-done | bytes 524320 | tf_op jit(solution)/shard_map/all_to_all | solution.py:14
  193.5 19.8 %all_to_all.60 = f32[8,32,512]{2,1,0:T(8,128)S(1)} all-to-all(f32[8,32,512]{2,1,0:T(8,128)S(1)} %copy.114), channel_id=1, replica_groups=mesh['y'=4,'core'=2,'z'=8,'x'=4] {'z'}, dimensions={0} | all-to-all | bytes 1048576 | tf_op jit(solution)/shard_map/all_to_all | solution.py:14
  213.3 2.1 broadcast_in_dim.14
  215.4 3.8 %all-to-all-start.10 = ((f32[2,4,32,8,128]{4,3,2,1,0:T(8,128)}), f32[2,4,32,8,128]{4,3,2,1,0:T(8,128)S(1)}, u32[]{:S(2)}, u32[]{:S(2)}) async-start(f32[2,4,32,8,128]{4,3,2,1,0:T(8,128)} %broadcast_in_dim.14), calls=%async_computation.10 | async-start | bytes 2097152 | tf_op jit(solution)/shard_map/all_to_all | solution.py:14
  219.4 1.9 all-to-all-done.10
  221.3 7.0 %convolution_bitcast_fusion.4 = f32[4,2,8,4]{2,3,0,1:T(4,128)S(1)} fusion(f32[2,4,32,8,128]{4,3,2,1,0:T(8,128)S(1)} %all-to-all-done.10, f32[32,4,128,1,1]{2,0,1,4,3:T(8,128)S(1)} %convolution_bitcast_fusion.3), kind=kOutput, calls=%fused_computation.17 | convolution fusion | flops 12582912 | bytes 1115136 | tf_op jit(solution)/shard_map/cykqj,kdj->ycqd/dot_general | solution.py:110
  228.4 12.8 %all_to_all.61 = f32[32,2,4]{2,1,0:T(2,128)S(1)} all-to-all(f32[32,2,4]{2,1,0:T(2,128)S(1)} %bitcast.101), channel_id=1, replica_groups=mesh['y'=4,'core'=2,'z'=8,'x'=4] {'z','x'}, dimensions={0} | all-to-all | bytes 2048 | tf_op jit(solution)/shard_map/all_to_all | solution.py:14
  (66 shorter events, 14.0 us)
Async XLA Ops:
  0.0 14.7 %copy-start = (bf16[2048,256]{1,0:T(8,128)(2,1)S(1)}, bf16[2048,256]{1,0:T(8,128)(2,1)}, u32[]{:S(2)}) copy-start(bf16[2048,256]{1,0:T(8,128)(2,1)} %param.10) | copy-start | bytes 3145732
  2.1 27.8 %all-to-all-start = ((f32[32,4,896]{2,1,0:T(4,128)}), f32[32,4,896]{2,1,0:T(4,128)S(1)}, u32[]{:S(2)}, u32[]{:S(2)}) async-start(f32[32,4,896]{2,1,0:T(4,128)} %bitcast.2), calls=%async_computation | async-start | bytes 917504 | tf_op jit(solution)/shard_map/all_to_all | solution.py:14
  30.0 4.3 %copy-start.5 = (f32[32,4,896]{2,1,0:T(4,128)}, f32[32,4,896]{2,1,0:T(4,128)S(1)}, u32[]{:S(2)}) copy-start(f32[32,4,896]{2,1,0:T(4,128)S(1)} %all-to-all-done) | copy-start | bytes 1376260
  30.2 4.0 %copy-start.7 = (f32[4,8,4,896]{3,2,1,0:T(4,128)}, f32[4,8,4,896]{3,2,1,0:T(4,128)S(1)}, u32[]{:S(2)}) copy-start(f32[4,8,4,896]{3,2,1,0:T(4,128)S(1)} %copy.102) | copy-start | bytes 1376260
  31.2 12.7 %collective-permute-start = (f32[128,896]{1,0:T(8,128)}, f32[128,896]{1,0:T(8,128)}, u32[]{:S(2)}, u32[]{:S(2)}) collective-permute-start(f32[128,896]{1,0:T(8,128)} %reshape.176), channel_id=1, source_target_pairs={{64,0},{128,64},{192,128},{0,192},{65,1},{129,65},{193,129},{1,193... | collective-permute-start | bytes 1376264 | tf_op jit(solution)/shard_map/ppermute | solution.py:23
  31.7 20.6 %collective-permute-start.1 = (f32[128,896]{1,0:T(8,128)}, f32[128,896]{1,0:T(8,128)}, u32[]{:S(2)}, u32[]{:S(2)}) collective-permute-start(f32[128,896]{1,0:T(8,128)} %reshape.176), channel_id=1, source_target_pairs={{128,0},{192,64},{0,128},{64,192},{129,1},{193,65},{1,129},{65,193... | collective-permute-start | bytes 1376264 | tf_op jit(solution)/shard_map/ppermute | solution.py:23
  34.3 18.9 %collective-permute-start.2 = (f32[128,896]{1,0:T(8,128)}, f32[128,896]{1,0:T(8,128)}, u32[]{:S(2)}, u32[]{:S(2)}) collective-permute-start(f32[128,896]{1,0:T(8,128)} %reshape.176), channel_id=1, source_target_pairs={{192,0},{0,64},{64,128},{128,192},{193,1},{1,65},{65,129},{129,193... | collective-permute-start | bytes 1376264 | tf_op jit(solution)/shard_map/ppermute | solution.py:23
  36.2 4.9 %copy-start.8 = (f32[4,8,4,896]{3,2,1,0:T(4,128)S(1)}, f32[4,8,4,896]{3,2,1,0:T(4,128)}, u32[]{:S(2)}) copy-start(f32[4,8,4,896]{3,2,1,0:T(4,128)} %copy-done.7) | copy-start | bytes 1376260
  37.6 18.2 %all-to-all-start.1 = ((f32[4,576,128]{2,1,0:T(8,128)}), f32[4,576,128]{2,1,0:T(8,128)S(1)}, u32[]{:S(2)}, u32[]{:S(2)}) async-start(f32[4,576,128]{2,1,0:T(8,128)} %bitcast.12), calls=%async_computation.1 | async-start | bytes 2359296 | tf_op jit(solution)/shard_map/all_to_all | solution.py:14
  41.2 19.5 %copy-start.12 = (s32[4]{0:T(128)S(1)}, s32[4]{0:T(128)}, u32[]{:S(2)}) copy-start(s32[4]{0:T(128)} %param.17) | copy-start | bytes 52
  41.4 36.8 %copy-start.6 = (f32[32,4,896]{2,1,0:T(4,128)S(1)}, f32[32,4,896]{2,1,0:T(4,128)}, u32[]{:S(2)}) copy-start(f32[32,4,896]{2,1,0:T(4,128)} %copy-done.5) | copy-start | bytes 1376260
  55.8 41.4 %collective-permute-start.3 = (f32[4,128,896]{2,1,0:T(8,128)}, f32[4,128,896]{2,1,0:T(8,128)}, u32[]{:S(2)}, u32[]{:S(2)}) collective-permute-start(f32[4,128,896]{2,1,0:T(8,128)} %pad_maximum_fusion), channel_id=1, source_target_pairs={{32,0},{0,32},{33,1},{1,33},{34,2},{2,34},{35,3},{3,35},{36,4},{4,... | collective-permute-start | bytes 5505032 | tf_op jit(solution)/shard_map/ppermute | solution.py:23
  56.6 17.3 %all-to-all-start.2 = ((f32[8,72,128]{2,1,0:T(8,128)}), f32[8,72,128]{2,1,0:T(8,128)S(1)}, u32[]{:S(2)}, u32[]{:S(2)}) async-start(f32[8,72,128]{2,1,0:T(8,128)} %bitcast.13), calls=%async_computation.2 | async-start | bytes 589824 | tf_op jit(solution)/shard_map/all_to_all | solution.py:14
  74.7 16.4 %all-to-all-start.3 = ((f32[8,72,128]{2,1,0:T(8,128)}), f32[8,72,128]{2,1,0:T(8,128)S(1)}, u32[]{:S(2)}, u32[]{:S(2)}) async-start(f32[8,72,128]{2,1,0:T(8,128)} %broadcast_in_dim.10), calls=%async_computation.3 | async-start | bytes 589824 | tf_op jit(solution)/shard_map/all_to_all | solution.py:14
  92.3 20.8 %all-to-all-start.4 = ((f32[4,576,128]{2,1,0:T(8,128)}), f32[4,576,128]{2,1,0:T(8,128)S(1)}, u32[]{:S(2)}, u32[]{:S(2)}) async-start(f32[4,576,128]{2,1,0:T(8,128)} %broadcast_in_dim.12), calls=%async_computation.4 | async-start | bytes 2359296 | tf_op jit(solution)/shard_map/all_to_all | solution.py:14
  97.2 2.8 %copy-start.1 = (f32[8,4,8,4,896]{4,2,3,1,0:T(8,128)S(1)}, f32[8,4,8,4,896]{4,2,3,1,0:T(8,128)}, u32[]{:S(2)}) copy-start(f32[8,4,8,4,896]{4,2,3,1,0:T(8,128)} %copy_dynamic-update-slice_fusion.1) | copy-start | bytes 11010052
  97.2 5.2 %copy-start.9 = (bf16[256,896]{1,0:T(8,128)(2,1)S(1)}, bf16[256,896]{1,0:T(8,128)(2,1)}, u32[]{:S(2)}) copy-start(bf16[256,896]{1,0:T(8,128)(2,1)} %param.11) | copy-start | bytes 1376260
  100.6 1.8 copy-start.2
  103.7 12.9 %copy-start.11 = (s32[2048]{0:T(1024)S(1)}, s32[2048]{0:T(1024)}, u32[]{:S(2)}) copy-start(s32[2048]{0:T(1024)} %param.16) | copy-start | bytes 24580
  113.1 14.6 %copy-start.4 = (f32[4,576,128]{2,1,0:T(8,128)}, f32[4,576,128]{2,1,0:T(8,128)S(1)}, u32[]{:S(2)}) copy-start(f32[4,576,128]{2,1,0:T(8,128)S(1)} %all-to-all-done.4) | copy-start | bytes 3538948
  113.1 17.9 %all-to-all-start.7 = ((f32[4,256,256]{2,1,0:T(8,128)}), f32[4,256,256]{2,1,0:T(8,128)S(1)}, u32[]{:S(2)}, u32[]{:S(2)}) async-start(f32[4,256,256]{2,1,0:T(8,128)} %copy.117), calls=%async_computation.7 | async-start | bytes 2097152 | tf_op jit(solution)/shard_map/all_to_all | solution.py:14
  132.1 18.5 %all-to-all-start.8 = ((f32[8,32,256]{2,1,0:T(8,128)}), f32[8,32,256]{2,1,0:T(8,128)S(1)}, u32[]{:S(2)}, u32[]{:S(2)}) async-start(f32[8,32,256]{2,1,0:T(8,128)} %copy.119), calls=%async_computation.8 | async-start | bytes 524288 | tf_op jit(solution)/shard_map/all_to_all | solution.py:14
  135.7 8.0 %copy-start.3 = (f32[8,4,8,4,896]{4,2,3,1,0:T(8,128)S(1)}, f32[8,4,8,4,896]{4,2,3,1,0:T(8,128)}, u32[]{:S(2)}) copy-start(f32[8,4,8,4,896]{4,2,3,1,0:T(8,128)} %copy-done.2) | copy-start | bytes 11010052
  148.6 5.6 %copy-start.10 = (f32[32,128]{1,0:T(8,128)S(1)}, f32[32,128]{1,0:T(8,128)}, u32[]{:S(2)}) copy-start(f32[32,128]{1,0:T(8,128)} %param.15) | copy-start | bytes 49156
  150.5 28.4 %all-to-all-start.5 = ((f32[4,256,512]{2,1,0:T(8,128)}), f32[4,256,512]{2,1,0:T(8,128)S(1)}, u32[]{:S(2)}, u32[]{:S(2)}) async-start(f32[4,256,512]{2,1,0:T(8,128)} %copy.112), calls=%async_computation.5 | async-start | bytes 4194304 | tf_op jit(solution)/shard_map/all_to_all | solution.py:14
  179.8 13.7 %all-to-all-start.9 = ((f32[4,32,8,128]{3,2,1,0:T(8,128)}), f32[4,32,8,128]{3,2,1,0:T(8,128)}, u32[]{:S(2)}, u32[]{:S(2)}) async-start(f32[4,32,8,128]{3,2,1,0:T(8,128)} %broadcast_in_dim.13), calls=%async_computation.9 | async-start | bytes 1048576 | tf_op jit(solution)/shard_map/all_to_all | solution.py:14
  215.4 5.9 %all-to-all-start.10 = ((f32[2,4,32,8,128]{4,3,2,1,0:T(8,128)}), f32[2,4,32,8,128]{4,3,2,1,0:T(8,128)S(1)}, u32[]{:S(2)}, u32[]{:S(2)}) async-start(f32[2,4,32,8,128]{4,3,2,1,0:T(8,128)} %broadcast_in_dim.14), calls=%async_computation.10 | async-start | bytes 2097152 | tf_op jit(solution)/shard_map/all_to_all | solution.py:14
